TPU v7x, 128 devices: a whole 4x4x4 slice. The times are simulated.
128 devices in a mesh: pool: 2 (over core), grp: 4 (over y), rep: 16 (over x, z).
Axes of the slice: x: 4, y: 4, z: 4, core: 2. Of those that a mesh axis runs over, the one named last changes fastest.
Arguments:
- queries: bfloat16 [512, 8192], P('pool', 'grp'), may hold values from -64 to 64
- keys: bfloat16 [16384, 512], P('rep', 'grp'), may hold values from -7 to 7
- values: bfloat16 [16384, 512], P('rep', 'grp'), may hold values from -6 to 6
- hidden_in: bfloat16 [512, 4096], P(('pool', 'grp', 'rep')), may hold values from -4 to 4
- o_weight: bfloat16 [8192, 4096], P('grp', 'rep'), may hold values from -0.125 to 0.125
- norm_gain: bfloat16 [4096], replicated, may hold values from 0.5 to 1.5
- routes: int32 [512, 8], P(('pool', 'grp', 'rep')), may hold values from 0 to 63, as said below
- route_weights: float32 [512, 8], P(('pool', 'grp', 'rep')), may hold values from 0.02 to 0.25
- w_gate: bfloat16 [64, 4096, 1536], P(('grp', 'rep'), None, 'pool'), may hold values from -0.09375 to 0.09375
- w_up: bfloat16 [64, 4096, 1536], P(('grp', 'rep'), None, 'pool'), may hold values from -0.09375 to 0.09375
- w_down: bfloat16 [64, 1536, 4096], P(('grp', 'rep'), 'pool'), may hold values from -0.15625 to 0.15625
Outputs:
- mid_rows: bfloat16 [512, 4096], P(('pool', 'grp', 'rep'))
- expert_mix: bfloat16 [512, 4096], P(('pool', 'grp', 'rep'))
Inputs may be any that keep to these rules, and one draw needn't show every extreme that they name: `routes`: each row names 8 different experts. In the rows of one device each expert is named by no row or by exactly 2 rows, and one expert, the same on every device, is named by 2 rows on every device.
All inputs are finite; a program needn't handle non-finite values.
Results may differ from a plain program's by a relative error of at most 0.027.
Values may be sent and summed in bfloat16 or wider, within the bound.
A program may use at most 128 MiB of HBM per device.

v0:
```python
import jax
import jax.numpy as jnp
from jax import lax
from jax.sharding import PartitionSpec as P

HEAD_DIM = 128


def expert_apply(rows_in, gate_w, up_w, down_w):
    gate_proj = jnp.dot(rows_in, gate_w, preferred_element_type=jnp.float32)
    upper = jnp.dot(rows_in, up_w, preferred_element_type=jnp.float32)
    activated = (jax.nn.silu(gate_proj) * upper).astype(jnp.bfloat16)
    return jnp.dot(activated, down_w, preferred_element_type=jnp.float32)


def per_device(
    queries,
    keys,
    values,
    hidden_in,
    o_weight,
    norm_gain,
    routes,
    route_weights,
    w_gate,
    w_up,
    w_down,
):
    kv_local = keys.shape[1] // HEAD_DIM
    heads_local = queries.shape[1] // HEAD_DIM
    group_size = heads_local // kv_local
    batch_rows = queries.shape[0]
    key_span = keys.shape[0]
    per_block = min(4, group_size)
    blocks = group_size // per_block
    score_scale = HEAD_DIM ** (-0.5)
    query_blocks = jnp.moveaxis(
        queries.reshape(batch_rows, kv_local, blocks, per_block, HEAD_DIM), 2, 0
    )
    key_heads = keys.reshape(key_span, kv_local, HEAD_DIM)
    value_heads = values.reshape(key_span, kv_local, HEAD_DIM)

    def local_part(query_block):
        scores = (
            jnp.einsum("rkhd,pkd->rkhp", query_block, key_heads, preferred_element_type=jnp.float32)
            * score_scale
        )
        top_score = jnp.max(scores, axis=-1)
        exp_scores = jnp.exp(scores - top_score[..., None])
        exp_total = jnp.sum(exp_scores, axis=-1)
        weighted = jnp.einsum(
            "rkhp,pkd->rkhd",
            exp_scores.astype(jnp.bfloat16),
            value_heads,
            preferred_element_type=jnp.float32,
        )
        return (top_score, exp_total, weighted)

    top_part, total_part, value_part = lax.map(local_part, query_blocks)
    rep_size = lax.axis_size("rep")
    share = batch_rows // rep_size
    rows_heads = share * heads_local

    def by_peer(part):
        part = jnp.moveaxis(part, 0, 2)
        return part.reshape((rep_size, rows_heads) + part.shape[4:])

    stats = jnp.stack([by_peer(top_part), by_peer(total_part)], axis=1)
    payload = jnp.concatenate([by_peer(value_part), stats.reshape(rep_size, -1, HEAD_DIM)], axis=1)
    payload = lax.all_to_all(payload, "rep", split_axis=0, concat_axis=0, tiled=True)
    weighted = payload[:, :rows_heads]
    stats = payload[:, rows_heads:].reshape(rep_size, 2, rows_heads)
    joint_top = jnp.max(stats[:, 0], axis=0)
    factors = jnp.exp(stats[:, 0] - joint_top)
    exp_total = jnp.sum(stats[:, 1] * factors, axis=0)
    weighted = jnp.sum(weighted * factors[..., None], axis=0)
    attention = (weighted / exp_total[:, None]).astype(jnp.bfloat16)
    attention = lax.all_gather(
        attention.reshape(share, heads_local * HEAD_DIM), "rep", axis=0, tiled=True
    )
    head_total = lax.psum_scatter(
        jnp.dot(attention, o_weight, preferred_element_type=jnp.float32),
        "grp",
        scatter_dimension=0,
        tiled=True,
    )
    attn_proj = head_total.astype(jnp.bfloat16)
    full_rows = lax.all_to_all(attn_proj, "rep", split_axis=0, concat_axis=1, tiled=True)
    mid_rows = (hidden_in.astype(jnp.float32) + full_rows.astype(jnp.float32)).astype(jnp.bfloat16)
    mid_wide = lax.optimization_barrier(mid_rows).astype(jnp.float32)
    inverse = lax.rsqrt(jnp.mean(mid_wide * mid_wide, axis=-1, keepdims=True) + 1e-06)
    normed = (mid_wide * inverse * norm_gain.astype(jnp.float32)).astype(jnp.bfloat16)
    row_dev, topk = routes.shape
    model_width = hidden_in.shape[1]
    group_count = lax.axis_size("grp")
    rep_count = lax.axis_size("rep")
    experts = group_count * rep_count
    capacity = max(2, 2 * row_dev * topk // experts)
    flat_routes = routes.reshape(-1)
    order = jnp.arange(flat_routes.shape[0], dtype=jnp.int32)
    same_before = (flat_routes[:, None] == flat_routes[None, :]) & (order[None, :] < order[:, None])
    position = jnp.sum(same_before.astype(jnp.int32), axis=1)
    slot_index = flat_routes * capacity + position
    chooser = jnp.any(
        jnp.arange(experts * capacity, dtype=jnp.int32)[:, None, None]
        == slot_index.reshape(row_dev, topk)[None, :, :],
        axis=2,
    ).astype(jnp.bfloat16)
    outgoing = jnp.dot(chooser, normed, preferred_element_type=jnp.float32).astype(jnp.bfloat16)
    arrived = lax.all_to_all(
        outgoing.reshape(experts, capacity, model_width),
        ("grp", "rep"),
        split_axis=0,
        concat_axis=0,
        tiled=True,
    )
    sources = arrived.shape[0]
    slots_here = arrived.shape[1]
    combined = expert_apply(
        lax.all_gather(arrived.reshape(-1, model_width), "pool", axis=0, tiled=True),
        w_gate[0],
        w_up[0],
        w_down[0],
    )
    served = (
        lax.psum_scatter(combined, "pool", scatter_dimension=0, tiled=True)
        .astype(jnp.bfloat16)
        .reshape(sources, slots_here, model_width)
    )
    returned = lax.all_to_all(served, ("grp", "rep"), split_axis=0, concat_axis=0, tiled=True)
    returned = returned.reshape(-1, model_width)
    picked = jnp.take(returned, slot_index, axis=0).reshape(row_dev, topk, model_width)
    expert_mix = jnp.sum(route_weights[..., None] * picked.astype(jnp.float32), axis=1).astype(
        jnp.bfloat16
    )
    return (mid_rows, expert_mix)


def solution(mesh):
    return jax.shard_map(
        per_device,
        mesh=mesh,
        in_specs=(
            P("pool", "grp"),
            P("rep", "grp"),
            P("rep", "grp"),
            P(("pool", "grp", "rep"), None),
            P("grp", "rep"),
            P(),
            P(("pool", "grp", "rep"), None),
            P(("pool", "grp", "rep"), None),
            P(("grp", "rep"), None, "pool"),
            P(("grp", "rep"), None, "pool"),
            P(("grp", "rep"), "pool", None),
        ),
        out_specs=(P(("pool", "grp", "rep"), None), P(("pool", "grp", "rep"), None)),
        check_vma=False,
    )
```

profile of v0, /device:TPU:0, one launch (start us, length us, event | category | flops | bytes accessed | tf_op | source)
XLA Modules:
  0.0 256.5 jit_solution(1512416310897008572)
XLA Ops:
  7.3 1.6 copy.23
  8.8 17.8 %while.14 = (s32[]{:T(128)}, f32[4,256,1,4]{1,3,2,0:T(4,128)S(1)}, f32[4,256,1,4]{1,3,2,0:T(4,128)S(1)}, f32[4,256,1,4,128]{4,1,3,2,0:T(8,128)}, bf16[4,256,1,4,...) while((s32[]{:T(128)}, f32[4,256,1,4]{1,3,2,0:T(4,128)S(1)}, ...), condition=%wide.region_3.4_spmd, body=%wide.region_0.3_spmd.sunk | while | flops 545257472 | bytes 14975609 | solution.py:59
  8.8 1.8 bitcast_reduce_fusion.2
  10.7 0.9 fusion.67
  11.6 1.6 fusion.68
  13.3 1.8 bitcast_reduce_fusion.2
  15.1 0.9 fusion.67
  16.0 1.7 fusion.68
  17.7 1.8 bitcast_reduce_fusion.2
  19.5 0.9 fusion.67
  20.5 1.7 fusion.68
  22.1 1.8 bitcast_reduce_fusion.2
  23.9 0.9 fusion.67
  24.9 1.7 fusion.68
  26.6 0.3 copy.26
  26.8 0.5 stack_reshape.6
  27.3 0.3 copy.27
  27.6 0.5 stack_reshape.7
  28.2 2.9 %copy.25 = f32[256,1,4,4,128]{4,3,2,0,1:T(4,128)S(1)} copy(f32[256,1,4,4,128]{4,0,3,1,2:T(8,128)} %bitcast.21) | data formatting | bytes 4194304 | tf_op jit(solution)/shard_map/transpose | solution.py:65
  31.1 0.2 pad_maximum_fusion
  31.3 37.1 %all_to_all.28 = f32[16,260,128]{2,1,0:T(8,128)S(1)} all-to-all(f32[16,260,128]{2,1,0:T(8,128)S(1)} %pad_maximum_fusion), channel_id=1, replica_groups=mesh['pool'=2,'grp'=4,'rep'=16] {'rep'}, dimensions={0} | all-to-all | bytes 4259840 | tf_op jit(solution)/shard_map/all_to_all | solution.py:70
  68.5 0.7 fusion.27
  69.4 0.7 fusion.37
  70.2 40.9 %all-gather.3.cloned.1.call-done = bf16[256,2048]{1,0:T(8,128)(2,1)} async-done(((bf16[16,2048]{1,0:T(8,128)(2,1)}), bf16[256,2048]{1,0:T(8,128)(2,1)}) %all-gather.3.cloned.1.call-update) | async-done | bytes 1048592 | tf_op jit(solution)/shard_map/all_gather | solution.py:78
  111.1 2.4 fusion.55
  113.6 0.2 convert_reduce_fusion
  113.9 19.6 %reduce-scatter.3.cloned.1.call-done = f32[64,256]{1,0:T(8,128)} async-done(((f32[256,256]{1,0:T(8,128)}), f32[64,256]{1,0:T(8,128)}) %reduce-scatter.3.cloned.1.call-update) | async-done | bytes 65552 | tf_op jit(solution)/shard_map/reduce_scatter | solution.py:81
  133.5 0.8 convert_element_type.55
  134.4 0.6 all_to_all.20
  135.0 6.9 %all-to-all-start.1 = ((bf16[16,4,256]{2,1,0:T(4,128)(2,1)}), bf16[16,4,256]{2,1,0:T(4,128)(2,1)S(1)}, u32[]{:S(2)}, u32[]{:S(2)}) async-start(bf16[16,4,256]{2,1,0:T(4,128)(2,1)} %all_to_all.20), calls=%async_computation.2 | async-start | bytes 65536 | tf_op jit(solution)/shard_map/all_to_all | solution.py:88
  142.1 7.5 %all-to-all-done.1 = bf16[16,4,256]{2,1,0:T(4,128)(2,1)S(1)} async-done(((bf16[16,4,256]{2,1,0:T(4,128)(2,1)}), bf16[16,4,256]{2,1,0:T(4,128)(2,1)S(1)}, u32[]{:S(2)}, u32[]{:S(2)}) %all-to-all-start.1) | async-done | bytes 32800 | tf_op jit(solution)/shard_map/all_to_all | solution.py:88
  149.6 0.1 fusion.38
  149.8 0.5 convolution_convert_fusion
  150.3 0.7 reshape.157
  151.0 20.0 %all_to_all.29 = bf16[64,2,4096]{2,1,0:T(2,128)(2,1)S(1)} all-to-all(bf16[64,2,4096]{2,1,0:T(2,128)(2,1)S(1)} %reshape.157), channel_id=1, replica_groups=mesh['pool'=2,'grp'=4,'rep'=16] {'grp','rep'}, dimensions={0} | all-to-all | bytes 2097152 | tf_op jit(solution)/shard_map/all_to_all | solution.py:110
  171.0 1.2 reshape.158
  172.3 0.2 reduce-scatter.5.cloned.1.call-start
  172.5 8.8 %all-gather.5.cloned.1.call-done = bf16[256,4096]{1,0:T(8,128)(2,1)} async-done(((bf16[128,4096]{1,0:T(8,128)(2,1)}), bf16[256,4096]{1,0:T(8,128)(2,1)}) %all-gather.5.cloned.1.call-update) | async-done | bytes 2097168 | tf_op jit(solution)/shard_map/all_gather | solution.py:120
  181.3 6.2 %fusion.25 = f32[256,768]{1,0:T(8,128)} fusion(bf16[256,4096]{1,0:T(8,128)(2,1)} %all-gather.5.cloned.1.call-done, bf16[1,4096,768]{2,1,0:T(8,128)(2,1)} %param.21), kind=kOutput, calls=%fused_computation.25 | convolution fusion | flops 1610612736 | bytes 9175040 | tf_op jit(solution)/shard_map/dot_general | solution.py:10
  187.5 11.3 %fusion.21 = f32[256,4096]{1,0:T(8,128)} fusion(bf16[1,768,4096]{2,1,0:T(8,128)(2,1)} %param.23, bf16[256,4096]{1,0:T(8,128)(2,1)S(1)} %copy-done.7, bf16[1,4096,768]{2,1,0:T(8,128)(2,1)} %param.22, f32[256,768]{1,0:T(8,128)} %fusion.25), kind=kOutput, calls=%fused_computation.21 | convolution fusion | flops 3222405120 | bytes 19660800 | tf_op jit(solution)/shard_map/dot_general | solution.py:13
  198.9 16.4 %reduce-scatter.5.cloned.1.call-done = f32[128,4096]{1,0:T(8,128)} async-done(((f32[256,4096]{1,0:T(8,128)}), f32[128,4096]{1,0:T(8,128)}) %reduce-scatter.5.cloned.1.call-update) | async-done | bytes 2097168 | tf_op jit(solution)/shard_map/reduce_scatter | solution.py:126
  215.2 1.7 convert_element_type.66
  217.0 1.5 reshape.159
  218.5 10.4 %all-to-all-start.3 = ((bf16[64,2,4096]{2,1,0:T(2,128)(2,1)}), bf16[64,2,4096]{2,1,0:T(2,128)(2,1)S(1)}, u32[]{:S(2)}, u32[]{:S(2)}) async-start(bf16[64,2,4096]{2,1,0:T(2,128)(2,1)} %reshape.159), calls=%async_computation.5 | async-start | bytes 2097152 | tf_op jit(solution)/shard_map/all_to_all | solution.py:130
  229.0 18.9 %all-to-all-done.3 = bf16[64,2,4096]{2,1,0:T(2,128)(2,1)S(1)} async-done(((bf16[64,2,4096]{2,1,0:T(2,128)(2,1)}), bf16[64,2,4096]{2,1,0:T(2,128)(2,1)S(1)}, u32[]{:S(2)}, u32[]{:S(2)}) %all-to-all-start.3) | async-done | bytes 1048608 | tf_op jit(solution)/shard_map/all_to_all | solution.py:130
  247.9 0.4 reshape.160
  248.4 0.7 gather_fusion
  249.1 0.9 multiply_reduce_fusion
  (58 shorter events, 1.1 us)
Async XLA Ops:
  7.2 104.0 %copy-start = (bf16[2048,256]{1,0:T(8,128)(2,1)S(1)}, bf16[2048,256]{1,0:T(8,128)(2,1)}, u32[]{:S(2)}) copy-start(bf16[2048,256]{1,0:T(8,128)(2,1)} %param.17) | copy-start | bytes 3145732
  7.2 103.9 %all-gather.3.cloned.1.call-start = ((), (), s32[]{:S(2)}) async-start(), calls=%async_computation.6 | async-start | bytes 1114112 | tf_op jit(solution)/shard_map/all_gather | solution.py:78
  8.8 2.8 %copy-start.1 = (bf16[1024,1,128]{2,0,1:T(8,128)(2,1)S(1)}, bf16[1024,1,128]{2,0,1:T(8,128)(2,1)}, u32[]{:S(2)}) copy-start(bf16[1024,1,128]{2,0,1:T(8,128)(2,1)} %get-tuple-element.156) | copy-start | bytes 786436 | tf_op jit(solution)/shard_map/while
  13.3 2.8 %copy-start.1 = (bf16[1024,1,128]{2,0,1:T(8,128)(2,1)S(1)}, bf16[1024,1,128]{2,0,1:T(8,128)(2,1)}, u32[]{:S(2)}) copy-start(bf16[1024,1,128]{2,0,1:T(8,128)(2,1)} %get-tuple-element.156) | copy-start | bytes 786436 | tf_op jit(solution)/shard_map/while
  17.7 2.8 %copy-start.1 = (bf16[1024,1,128]{2,0,1:T(8,128)(2,1)S(1)}, bf16[1024,1,128]{2,0,1:T(8,128)(2,1)}, u32[]{:S(2)}) copy-start(bf16[1024,1,128]{2,0,1:T(8,128)(2,1)} %get-tuple-element.156) | copy-start | bytes 786436 | tf_op jit(solution)/shard_map/while
  22.1 2.8 %copy-start.1 = (bf16[1024,1,128]{2,0,1:T(8,128)(2,1)S(1)}, bf16[1024,1,128]{2,0,1:T(8,128)(2,1)}, u32[]{:S(2)}) copy-start(bf16[1024,1,128]{2,0,1:T(8,128)(2,1)} %get-tuple-element.156) | copy-start | bytes 786436 | tf_op jit(solution)/shard_map/while
  31.3 82.3 %copy-start.4 = (s32[4,8]{1,0:T(4,128)S(1)}, s32[4,8]{1,0:T(4,128)}, u32[]{:S(2)}) copy-start(s32[4,8]{1,0:T(4,128)} %param.19) | copy-start | bytes 388
  31.3 110.8 %copy-start.5 = (bf16[4096]{0:T(1024)(128)(2,1)S(1)}, bf16[4096]{0:T(1024)(128)(2,1)}, u32[]{:S(2)}) copy-start(bf16[4096]{0:T(1024)(128)(2,1)} %param.18) | copy-start | bytes 24580
  68.4 81.2 %copy-start.3 = (bf16[4,4096]{1,0:T(4,128)(2,1)S(1)}, bf16[4,4096]{1,0:T(4,128)(2,1)}, u32[]{:S(2)}) copy-start(bf16[4,4096]{1,0:T(4,128)(2,1)} %param.16) | copy-start | bytes 98308
  70.2 63.4 %reduce-scatter.3.cloned.1.call-start = ((), (), s32[]{:S(2)}) async-start(), calls=%async_computation.7 | async-start | bytes 327680 | tf_op jit(solution)/shard_map/reduce_scatter | solution.py:81
  135.0 14.6 %all-to-all-start.1 = ((bf16[16,4,256]{2,1,0:T(4,128)(2,1)}), bf16[16,4,256]{2,1,0:T(4,128)(2,1)S(1)}, u32[]{:S(2)}, u32[]{:S(2)}) async-start(bf16[16,4,256]{2,1,0:T(4,128)(2,1)} %all_to_all.20), calls=%async_computation.2 | async-start | bytes 65536 | tf_op jit(solution)/shard_map/all_to_all | solution.py:88
  142.0 39.4 %all-gather.5.cloned.1.call-start = ((), (), s32[]{:S(2)}) async-start(), calls=%async_computation.8 | async-start | bytes 3145728 | tf_op jit(solution)/shard_map/all_gather | solution.py:120
  149.6 22.6 %copy-start.2 = (bf16[4,4096]{1,0:T(4,128)(2,1)}, bf16[4,4096]{1,0:T(4,128)(2,1)S(1)}, u32[]{:S(2)}) copy-start(bf16[4,4096]{1,0:T(4,128)(2,1)S(1)} %add_convert_fusion) | copy-start | bytes 98308
  172.3 43.0 %reduce-scatter.5.cloned.1.call-start = ((), (), s32[]{:S(2)}) async-start(), calls=%async_computation.9 | async-start | bytes 6291456 | tf_op jit(solution)/shard_map/reduce_scatter | solution.py:126
  181.3 6.2 %copy-start.7 = (bf16[256,4096]{1,0:T(8,128)(2,1)S(1)}, bf16[256,4096]{1,0:T(8,128)(2,1)}, u32[]{:S(2)}) copy-start(bf16[256,4096]{1,0:T(8,128)(2,1)} %all-gather.5.cloned.1.call-done) | copy-start | bytes 6291460
  217.0 32.1 %copy-start.6 = (f32[4,8]{1,0:T(4,128)S(1)}, f32[4,8]{1,0:T(4,128)}, u32[]{:S(2)}) copy-start(f32[4,8]{1,0:T(4,128)} %param.20) | copy-start | bytes 388
  218.5 29.4 %all-to-all-start.3 = ((bf16[64,2,4096]{2,1,0:T(2,128)(2,1)}), bf16[64,2,4096]{2,1,0:T(2,128)(2,1)S(1)}, u32[]{:S(2)}, u32[]{:S(2)}) async-start(bf16[64,2,4096]{2,1,0:T(2,128)(2,1)} %reshape.159), calls=%async_computation.5 | async-start | bytes 2097152 | tf_op jit(solution)/shard_map/all_to_all | solution.py:130
Sparse Core Ops, SparseCore 0:
  70.3 40.8 all-gather.2
  113.6 19.8 reduce-scatter.2
  172.4 8.9 all-gather.4
  199.0 16.1 reduce-scatter.4
where the time goes:
time: 257 us; the launch traced here: 256 us
  waiting for transfers between devices  112 us (44%)
  blocking collectives  57.1 us (22%)
  matrix products  34.3 us (13%)
  starting transfers between devices  17.7 us (7%)
  between operations  14 us (5%)
  local copies, waits for them, and re-layouts  11.9 us (5%)
  other arithmetic  9.24 us (4%)
    all_gather x1, waiting for transfers between devices, per_device(): lax.all_gather(attention.reshape(share, heads_local * HEAD_DIM), 'rep', a...  40.9 us
    all_to_all x1, blocking collectives, per_device(): lax.all_to_all(payload, 'rep', split_axis=0, concat_axis=0, tiled=True)  37.1 us
    all_to_all x1, blocking collectives, per_device(): lax.all_to_all(outgoing.reshape(experts, capacity, model_width), ('grp',...  20 us
    reduce_scatter x1, waiting for transfers between devices, per_device(): lax.psum_scatter(jnp.dot(attention, o_weight, preferred_element_type=jnp....  19.6 us
    all_to_all x1, waiting for transfers between devices, per_device(): lax.all_to_all(served, ('grp', 'rep'), split_axis=0, concat_axis=0, tiled...  18.9 us
    reduce_scatter x1, waiting for transfers between devices, per_device(): lax.psum_scatter(combined, 'pool', scatter_dimension=0, tiled=True)  16.4 us
    dot_general x1, matrix products, expert_apply(): return jnp.dot(activated, down_w, preferred_element_type=jnp.float32)  11.3 us
    all_to_all x1, starting transfers between devices, per_device(): lax.all_to_all(served, ('grp', 'rep'), split_axis=0, concat_axis=0, tiled...  10.4 us
  transfers between devices with their start and end apart: 6, of which 6 were waited for; matrix products, arithmetic and copies ran while one was open for 0% of the time, Pallas kernels for 0%

commit v1 on v0

--- a/solution.py
+++ b/solution.py
@@ -117,7 +117,12 @@
     sources = arrived.shape[0]
     slots_here = arrived.shape[1]
     combined = expert_apply(
-        lax.all_gather(arrived.reshape(-1, model_width), "pool", axis=0, tiled=True),
+        jnp.concatenate(
+            lax.all_to_all(
+                jnp.stack([arrived.reshape(-1, model_width)] * lax.axis_size("pool")), "pool", 0, 0
+            ),
+            axis=0,
+        ),
         w_gate[0],
         w_up[0],
         w_down[0],

time: 257 us -> 248 us (0.965)
  waiting for transfers between devices: 112 us -> 97.7 us
  blocking collectives: 57.1 us -> 62.6 us
    all_gather x1 -> x0, waiting for transfers between devices: 8.83 us -> none  [per_device(): lax.all_gather(arrived.reshape(-1, model_width), 'pool', axis=0, tiled=True)]
    reduce_scatter x1, waiting for transfers between devices: 16.4 us -> 10.7 us  [per_device(): lax.psum_scatter(combined, 'pool', scatter_dimension=0, tiled=True)]
    all_to_all x0 -> x1, blocking collectives: none -> 5.42 us  [per_device(): lax.all_to_all(jnp.stack([arrived.reshape(-1, model_width)] * lax.axis_si...]
  transfers between devices with their start and end apart: 6 -> 5, of which waited for: 6 -> 5; matrix products, arithmetic and copies ran while one was open for 0% -> 0% of each run, Pallas kernels for 0% -> 0%
where the time goes in v1:
time: 248 us; the launch traced here: 247 us
  waiting for transfers between devices  97.7 us (39%)
  blocking collectives  62.6 us (25%)
  matrix products  33.4 us (13%)
  starting transfers between devices  17.5 us (7%)
  between operations  14 us (6%)
  local copies, waits for them, and re-layouts  12.1 us (5%)
  other arithmetic  9.41 us (4%)
    all_gather x1, waiting for transfers between devices, per_device(): lax.all_gather(attention.reshape(share, heads_local * HEAD_DIM), 'rep', a...  40.9 us
    all_to_all x1, blocking collectives, per_device(): lax.all_to_all(payload, 'rep', split_axis=0, concat_axis=0, tiled=True)  37.1 us
    all_to_all x1, blocking collectives, per_device(): lax.all_to_all(outgoing.reshape(experts, capacity, model_width), ('grp',...  20.1 us
    reduce_scatter x1, waiting for transfers between devices, per_device(): lax.psum_scatter(jnp.dot(attention, o_weight, preferred_element_type=jnp....  19.6 us
    all_to_all x1, waiting for transfers between devices, per_device(): lax.all_to_all(served, ('grp', 'rep'), split_axis=0, concat_axis=0, tiled...  18.9 us
    dot_general x1, matrix products, expert_apply(): return jnp.dot(activated, down_w, preferred_element_type=jnp.float32)  11.3 us
    reduce_scatter x1, waiting for transfers between devices, per_device(): lax.psum_scatter(combined, 'pool', scatter_dimension=0, tiled=True)  10.7 us
    all_to_all x1, starting transfers between devices, per_device(): lax.all_to_all(served, ('grp', 'rep'), split_axis=0, concat_axis=0, tiled...  10.4 us
  transfers between devices with their start and end apart: 5, of which 5 were waited for; matrix products, arithmetic and copies ran while one was open for 0% of the time, Pallas kernels for 0%

profile of v1, /device:TPU:0, one launch (start us, length us, event | category | flops | bytes accessed | tf_op | source)
XLA Modules:
  0.0 246.7 jit_solution(13135555480227552452)
XLA Ops:
  7.3 1.6 copy.23
  8.8 17.6 %while.14 = (s32[]{:T(128)}, f32[4,256,1,4]{1,3,2,0:T(4,128)S(1)}, f32[4,256,1,4]{1,3,2,0:T(4,128)S(1)}, f32[4,256,1,4,128]{4,1,3,2,0:T(8,128)}, bf16[4,256,1,4,...) while((s32[]{:T(128)}, f32[4,256,1,4]{1,3,2,0:T(4,128)S(1)}, ...), condition=%wide.region_3.4_spmd, body=%wide.region_0.3_spmd.sunk | while | flops 545257472 | bytes 14975609 | solution.py:59
  8.8 1.8 bitcast_reduce_fusion.2
  10.6 0.9 fusion.67
  11.6 1.6 fusion.68
  13.2 1.8 bitcast_reduce_fusion.2
  15.0 0.9 fusion.67
  15.9 1.7 fusion.68
  17.6 1.8 bitcast_reduce_fusion.2
  19.4 0.9 fusion.67
  20.3 1.7 fusion.68
  22.0 1.8 bitcast_reduce_fusion.2
  23.8 0.9 fusion.67
  24.7 1.7 fusion.68
  26.4 0.3 copy.26
  26.7 0.5 stack_reshape.10
  27.2 0.3 copy.27
  27.4 0.5 stack_reshape.11
  28.0 2.9 %copy.25 = f32[256,1,4,4,128]{4,3,2,0,1:T(4,128)S(1)} copy(f32[256,1,4,4,128]{4,0,3,1,2:T(8,128)} %bitcast.21) | data formatting | bytes 4194304 | tf_op jit(solution)/shard_map/transpose | solution.py:65
  31.0 0.2 pad_maximum_fusion
  31.1 37.1 %all_to_all.33 = f32[16,260,128]{2,1,0:T(8,128)S(1)} all-to-all(f32[16,260,128]{2,1,0:T(8,128)S(1)} %pad_maximum_fusion), channel_id=1, replica_groups=mesh['pool'=2,'grp'=4,'rep'=16] {'rep'}, dimensions={0} | all-to-all | bytes 4259840 | tf_op jit(solution)/shard_map/all_to_all | solution.py:70
  68.4 0.7 fusion.27
  69.3 0.7 fusion.37
  70.1 40.9 %all-gather.2.cloned.1.call-done = bf16[256,2048]{1,0:T(8,128)(2,1)} async-done(((bf16[16,2048]{1,0:T(8,128)(2,1)}), bf16[256,2048]{1,0:T(8,128)(2,1)}) %all-gather.2.cloned.1.call-update) | async-done | bytes 1048592 | tf_op jit(solution)/shard_map/all_gather | solution.py:78
  111.0 2.4 fusion.55
  113.5 0.2 convert_reduce_fusion
  113.8 19.6 %reduce-scatter.3.cloned.1.call-done = f32[64,256]{1,0:T(8,128)} async-done(((f32[256,256]{1,0:T(8,128)}), f32[64,256]{1,0:T(8,128)}) %reduce-scatter.3.cloned.1.call-update) | async-done | bytes 65552 | tf_op jit(solution)/shard_map/reduce_scatter | solution.py:81
  133.4 0.8 convert_element_type.55
  134.2 0.6 all_to_all.23
  134.9 7.0 %all-to-all-start.1 = ((bf16[16,4,256]{2,1,0:T(4,128)(2,1)}), bf16[16,4,256]{2,1,0:T(4,128)(2,1)S(1)}, u32[]{:S(2)}, u32[]{:S(2)}) async-start(bf16[16,4,256]{2,1,0:T(4,128)(2,1)} %all_to_all.23), calls=%async_computation.2 | async-start | bytes 65536 | tf_op jit(solution)/shard_map/all_to_all | solution.py:88
  142.0 7.5 %all-to-all-done.1 = bf16[16,4,256]{2,1,0:T(4,128)(2,1)S(1)} async-done(((bf16[16,4,256]{2,1,0:T(4,128)(2,1)}), bf16[16,4,256]{2,1,0:T(4,128)(2,1)S(1)}, u32[]{:S(2)}, u32[]{:S(2)}) %all-to-all-start.1) | async-done | bytes 32800 | tf_op jit(solution)/shard_map/all_to_all | solution.py:88
  149.5 0.1 fusion.38
  149.7 0.5 convolution_convert_fusion
  150.1 0.7 reshape.157
  150.9 20.1 %all_to_all.34 = bf16[64,2,4096]{2,1,0:T(2,128)(2,1)} all-to-all(bf16[64,2,4096]{2,1,0:T(2,128)(2,1)S(1)} %reshape.157), channel_id=1, replica_groups=mesh['pool'=2,'grp'=4,'rep'=16] {'grp','rep'}, dimensions={0} | all-to-all | bytes 2097152 | tf_op jit(solution)/shard_map/all_to_all | solution.py:110
  171.0 1.5 stack_reshape.12
  172.4 0.2 pad_maximum_fusion.1
  172.6 5.4 %all_to_all.35 = bf16[2,128,4096]{2,1,0:T(8,128)(2,1)S(1)} all-to-all(bf16[2,128,4096]{2,1,0:T(8,128)(2,1)S(1)} %pad_maximum_fusion.1), channel_id=1, replica_groups=mesh['pool'=2,'grp'=4,'rep'=16] {'pool'}, dimensions={0} | all-to-all | bytes 4194304 | tf_op jit(solution)/shard_map/all_to_all | solution.py:121
  178.1 5.4 %fusion.25 = f32[256,768]{1,0:T(8,128)} fusion(bf16[256,4096]{1,0:T(8,128)(2,1)S(1)} %bitcast.142, bf16[1,4096,768]{2,1,0:T(8,128)(2,1)} %param.21), kind=kOutput, calls=%fused_computation.25 | convolution fusion | flops 1610612736 | bytes 9175040 | tf_op jit(solution)/shard_map/dot_general | solution.py:10
  183.5 11.3 %fusion.21 = f32[256,4096]{1,0:T(8,128)} fusion(bf16[1,768,4096]{2,1,0:T(8,128)(2,1)} %param.23, bf16[256,4096]{1,0:T(8,128)(2,1)S(1)} %bitcast.143, bf16[1,4096,768]{2,1,0:T(8,128)(2,1)} %param.22, f32[256,768]{1,0:T(8,128)} %fusion.25), kind=kOutput, calls=%fused_computation.21 | convolution fusion | flops 3222405120 | bytes 19660800 | tf_op jit(solution)/shard_map/dot_general | solution.py:13
  194.8 10.7 %reduce-scatter.5.cloned.1.call-done = f32[128,4096]{1,0:T(8,128)} async-done(((f32[256,4096]{1,0:T(8,128)}), f32[128,4096]{1,0:T(8,128)}) %reduce-scatter.5.cloned.1.call-update) | async-done | bytes 2097168 | tf_op jit(solution)/shard_map/reduce_scatter | solution.py:131
  205.5 1.7 convert_element_type.66
  207.2 1.5 reshape.159
  208.8 10.4 %all-to-all-start.4 = ((bf16[64,2,4096]{2,1,0:T(2,128)(2,1)}), bf16[64,2,4096]{2,1,0:T(2,128)(2,1)S(1)}, u32[]{:S(2)}, u32[]{:S(2)}) async-start(bf16[64,2,4096]{2,1,0:T(2,128)(2,1)} %reshape.159), calls=%async_computation.6 | async-start | bytes 2097152 | tf_op jit(solution)/shard_map/all_to_all | solution.py:135
  219.3 18.9 %all-to-all-done.4 = bf16[64,2,4096]{2,1,0:T(2,128)(2,1)S(1)} async-done(((bf16[64,2,4096]{2,1,0:T(2,128)(2,1)}), bf16[64,2,4096]{2,1,0:T(2,128)(2,1)S(1)}, u32[]{:S(2)}, u32[]{:S(2)}) %all-to-all-start.4) | async-done | bytes 1048608 | tf_op jit(solution)/shard_map/all_to_all | solution.py:135
  238.2 0.4 reshape.160
  238.6 0.7 gather_fusion
  239.4 0.9 multiply_reduce_fusion
  (55 shorter events, 1.1 us)
Async XLA Ops:
  7.2 103.8 %copy-start = (bf16[2048,256]{1,0:T(8,128)(2,1)S(1)}, bf16[2048,256]{1,0:T(8,128)(2,1)}, u32[]{:S(2)}) copy-start(bf16[2048,256]{1,0:T(8,128)(2,1)} %param.17) | copy-start | bytes 3145732
  7.2 103.8 %all-gather.2.cloned.1.call-start = ((), (), s32[]{:S(2)}) async-start(), calls=%async_computation.7 | async-start | bytes 1114112 | tf_op jit(solution)/shard_map/all_gather | solution.py:78
  10.6 1.0 copy-start.1
  15.0 1.0 copy-start.1
  19.4 1.0 copy-start.1
  23.8 1.0 copy-start.1
  69.1 44.3 %copy-start.4 = (s32[4,8]{1,0:T(4,128)S(1)}, s32[4,8]{1,0:T(4,128)}, u32[]{:S(2)}) copy-start(s32[4,8]{1,0:T(4,128)} %param.19) | copy-start | bytes 388
  69.1 72.9 %copy-start.5 = (bf16[4096]{0:T(1024)(128)(2,1)S(1)}, bf16[4096]{0:T(1024)(128)(2,1)}, u32[]{:S(2)}) copy-start(bf16[4096]{0:T(1024)(128)(2,1)} %param.18) | copy-start | bytes 24580
  69.1 80.4 %copy-start.3 = (bf16[4,4096]{1,0:T(4,128)(2,1)S(1)}, bf16[4,4096]{1,0:T(4,128)(2,1)}, u32[]{:S(2)}) copy-start(bf16[4,4096]{1,0:T(4,128)(2,1)} %param.16) | copy-start | bytes 98308
  70.0 63.4 %reduce-scatter.3.cloned.1.call-start = ((), (), s32[]{:S(2)}) async-start(), calls=%async_computation.8 | async-start | bytes 327680 | tf_op jit(solution)/shard_map/reduce_scatter | solution.py:81
  134.9 14.6 %all-to-all-start.1 = ((bf16[16,4,256]{2,1,0:T(4,128)(2,1)}), bf16[16,4,256]{2,1,0:T(4,128)(2,1)S(1)}, u32[]{:S(2)}, u32[]{:S(2)}) async-start(bf16[16,4,256]{2,1,0:T(4,128)(2,1)} %all_to_all.23), calls=%async_computation.2 | async-start | bytes 65536 | tf_op jit(solution)/shard_map/all_to_all | solution.py:88
  141.8 63.7 %reduce-scatter.5.cloned.1.call-start = ((), (), s32[]{:S(2)}) async-start(), calls=%async_computation.9 | async-start | bytes 6291456 | tf_op jit(solution)/shard_map/reduce_scatter | solution.py:131
  149.5 21.5 %copy-start.2 = (bf16[4,4096]{1,0:T(4,128)(2,1)}, bf16[4,4096]{1,0:T(4,128)(2,1)S(1)}, u32[]{:S(2)}) copy-start(bf16[4,4096]{1,0:T(4,128)(2,1)S(1)} %add_convert_fusion) | copy-start | bytes 98308
  208.8 29.5 %all-to-all-start.4 = ((bf16[64,2,4096]{2,1,0:T(2,128)(2,1)}), bf16[64,2,4096]{2,1,0:T(2,128)(2,1)S(1)}, u32[]{:S(2)}, u32[]{:S(2)}) async-start(bf16[64,2,4096]{2,1,0:T(2,128)(2,1)} %reshape.159), calls=%async_computation.6 | async-start | bytes 2097152 | tf_op jit(solution)/shard_map/all_to_all | solution.py:135
  219.3 20.1 %copy-start.6 = (f32[4,8]{1,0:T(4,128)S(1)}, f32[4,8]{1,0:T(4,128)}, u32[]{:S(2)}) copy-start(f32[4,8]{1,0:T(4,128)} %param.20) | copy-start | bytes 388
Sparse Core Ops, SparseCore 0:
  70.1 40.7 all-gather.1
  113.5 19.8 reduce-scatter.2
  195.0 10.5 reduce-scatter.4
